TPU v7x, 32 devices: a whole 2x2x4 slice. The times are simulated.
32 devices in a mesh: runs: 2 (over y), ctx: 4 (over z), head: 4 (over x, core).
Axes of the slice: x: 2, y: 2, z: 4, core: 2. Of those that a mesh axis runs over, the one named last changes fastest.
Arguments:
- tokens: bfloat16 [4096, 2048], P(('runs', 'ctx', 'head')), parts along dimension 0, may hold values from -400 to 400
- in_gain: float32 [2048], replicated, may hold values from 0.1 to 1.9
- projections: bfloat16 [3, 2048, 2048], P(None, 'ctx', 'head'), may hold values from -0.125 to 0.125
- prior_state: float32 [32, 128, 128], P(('runs', 'head')), parts along dimension 0, may hold values from -256 to 256
- out_gain: float32 [2048], P('head'), may hold values from 0.1 to 1.9
Outputs:
- attended: bfloat16 [4096, 2048], P(('runs', 'ctx', 'head')), parts along dimension 0
There are 2 independent parts, one for each index of `runs`. A program takes and returns all parts, laid end to end along the dimension named above; an argument that names none is the same for every part. Nothing has to cross between parts.
All inputs are finite; a program needn't handle non-finite values.
Results may differ from a plain program's by a relative error of at most 0.0071.
Values may be sent and summed in bfloat16 or wider, within the bound.
A program may use at most 64 MiB of HBM per device.

v0:
```python
import jax
import jax.numpy as jnp
from jax import lax
from jax.sharding import PartitionSpec as P

BLOCK = 512


def prefix(part, axis, combine, identity):
    place = lax.axis_index(axis)
    gathered = lax.all_gather(part, axis)
    state = jnp.zeros_like(part) + jnp.asarray(identity, part.dtype)

    def one(step, state):
        return combine(state, lax.dynamic_index_in_dim(gathered, step, 0, False))

    return lax.fori_loop(0, place, one, state)


def rms_tokens(values_in, gain):
    wide = values_in.astype(jnp.float32)
    scale = lax.rsqrt(jnp.mean(wide * wide, axis=-1, keepdims=True) + 1e-06)
    return (wide * scale * gain).astype(jnp.bfloat16)


def combine_sum(earlier, later):
    return earlier + later


def on_device(tokens, in_gain, projections, prior_state, out_gain):
    normed = rms_tokens(tokens, in_gain)
    width_here = projections.shape[2]
    heads_here = prior_state.shape[0]
    head_dim = prior_state.shape[1]
    full_weights = lax.all_gather(projections, "ctx", axis=1, tiled=True)
    mapped = jnp.einsum(
        "td,jdc->jtc",
        lax.all_gather(normed, "head", axis=0, tiled=True),
        full_weights,
        preferred_element_type=jnp.float32,
    ).astype(jnp.bfloat16)
    span_rows = mapped.shape[1]
    blocks = span_rows // BLOCK
    shaped = mapped.reshape(3, blocks, BLOCK, heads_here, head_dim)
    queries = shaped[0]
    keys_all = shaped[1]
    values_all = shaped[2]
    block_states = jnp.einsum(
        "bkhd,bkhe->bhde", keys_all, values_all, preferred_element_type=jnp.float32
    )
    local_total = jnp.sum(block_states, axis=0)
    before = prefix(local_total, "ctx", combine_sum, jnp.zeros_like(local_total))
    entering = prior_state + before
    starts = entering[None] + jnp.cumsum(block_states, axis=0) - block_states
    position = jnp.arange(BLOCK, dtype=jnp.int32)
    causal = position[:, None] >= position[None, :]
    scores = jnp.einsum("bqhd,bkhd->bhqk", queries, keys_all, preferred_element_type=jnp.float32)
    scores = jnp.where(causal[None, None], scores, 0.0).astype(jnp.bfloat16)
    intra = jnp.einsum("bhqk,bkhd->bqhd", scores, values_all, preferred_element_type=jnp.float32)
    inter = jnp.einsum(
        "bqhd,bhde->bqhe", queries, starts.astype(jnp.bfloat16), preferred_element_type=jnp.float32
    )
    mixed = intra + inter
    scale = lax.rsqrt(jnp.mean(mixed * mixed, axis=-1, keepdims=True) + 1e-06)
    gains = out_gain.reshape(heads_here, head_dim)
    result = (mixed * scale * gains).astype(jnp.bfloat16).reshape(span_rows, width_here)
    return lax.all_to_all(result, "head", split_axis=0, concat_axis=1, tiled=True)


def solution(mesh):
    in_specs = (
        P(("runs", "ctx", "head"), None),
        P(),
        P(None, "ctx", "head"),
        P(("runs", "head"), None, None),
        P("head"),
    )
    out_specs = P(("runs", "ctx", "head"), None)
    return jax.shard_map(
        on_device, mesh=mesh, in_specs=in_specs, out_specs=out_specs, check_vma=False
    )
```

profile of v0, /device:TPU:0, one launch (start us, length us, event | category | flops | bytes accessed | tf_op | source)
XLA Modules:
  0.0 211.0 jit_solution(1581802129097191559)
XLA Ops:
  6.5 0.0 copy-start.1
  6.5 0.0 all-gather.5.cloned.1.call-start
  6.5 1.3 fusion.11
  7.9 2.0 fusion.13
  9.9 0.0 all-gather.5.cloned.1.call-update
  9.9 0.0 all-gather.7.cloned.1.call-start
  10.0 0.0 copy-done.1
  10.0 1.6 copy.11
  11.6 0.0 all-gather.7.cloned.1.call-update
  11.6 0.0 all-gather.9.cloned.1.call-start
  11.7 23.7 %all-gather.5.cloned.1.call-done = bf16[512,2048]{1,0:T(8,128)(2,1)} async-done(((bf16[128,2048]{1,0:T(8,128)(2,1)}), bf16[512,2048]{1,0:T(8,128)(2,1)}) %all-gather.5.cloned.1.call-update) | async-done | bytes 2097168 | tf_op jit(solution)/shard_map/all_gather | solution.py:38
  35.4 117.0 %all-gather.7.cloned.1.call-done = bf16[3,2048,512]{1,2,0:T(8,128)(2,1)} async-done(((bf16[3,512,512]{1,2,0:T(8,128)(2,1)}), bf16[3,2048,512]{1,2,0:T(8,128)(2,1)}) %all-gather.7.cloned.1.call-update) | async-done | bytes 6291472 | tf_op jit(solution)/shard_map/all_gather | solution.py:35
  152.3 6.9 %fusion.6 = bf16[3,512,512]{1,2,0:T(8,128)(2,1)S(1)} fusion(bf16[3,2048,512]{1,2,0:T(8,128)(2,1)} %all-gather.7.cloned.1.call-done, bf16[512,2048]{1,0:T(8,128)(2,1)} %all-gather.5.cloned.1.call-done), kind=kOutput, calls=%fused_computation.6 | convolution fusion | flops 3222011904 | bytes 9961472 | tf_op jit(solution)/shard_map/td,jdc->jtc/dot_general | solution.py:36
  159.2 0.1 fusion.18
  159.4 1.0 fusion.19
  160.4 0.0 all-gather.9.cloned.1.call-update
  160.4 0.1 iota_compare_fusion
  160.5 26.2 %all-gather.9.cloned.1.call-done = f32[16,128,128]{2,1,0:T(8,128)} async-done(((f32[4,128,128]{2,1,0:T(8,128)}), f32[16,128,128]{2,1,0:T(8,128)}) %all-gather.9.cloned.1.call-update) | async-done | bytes 1048592 | tf_op jit(solution)/shard_map/all_gather | solution.py:11
  186.7 0.0 copy-start
  186.7 0.0 copy-start.2
  186.7 0.9 copy-done
  187.6 0.1 copy-done.2
  187.7 1.3 fusion.15
  189.0 0.0 copy-start.3
  189.0 2.6 %multiply_reduce_fusion = (f32[512,4]{0,1:T(4,128)S(1)}, f32[1,512,4,128]{1,3,2,0:T(8,128)S(1)}) fusion(f32[4,128,512]{2,1,0:T(8,128)} %fusion.15, bf16[512,4,128]{0,2,1:T(8,128)(2,1)S(1)} %bitcast.38, bf16[512,4,128]{0,2,1:T(8,128)(2,1)S(1)} %bitcast.42, bf16[512,4,128]{0,2,1:T(8,128)(2,1)S(1)} %bitcast.40, pred[512,512]{1,0:T(8,128)(4,1)S(1)} %iota_compare_fusion), kind=kOutput, calls=%fused_computation.15 | convolution fusion | flops 539752448 | bytes 3940352 | tf_op jit(solution)/shard_map/bhqk,bkhd->bqhd/dot_general | solution.py:59
  191.7 0.0 copy-done.3
  191.7 0.2 multiply_convert_fusion
  191.9 0.1 all_to_all.14
  192.0 0.1 copy.15
  192.1 11.4 %all_to_all.19 = bf16[4,128,512]{1,2,0:T(8,128)(2,1)S(1)} all-to-all(bf16[4,128,512]{1,2,0:T(8,128)(2,1)S(1)} %copy.15), channel_id=1, replica_groups=mesh['runs'=2,'ctx'=4,'head'=4] {'head'}, dimensions={0} | all-to-all | bytes 1048576 | tf_op jit(solution)/shard_map/all_to_all | solution.py:67
  203.5 1.0 copy.16
  (4 shorter events, 0.0 us)
Async XLA Ops:
  6.5 3.5 %copy-start.1 = (bf16[3,512,512]{2,1,0:T(8,128)(2,1)S(1)}, bf16[3,512,512]{2,1,0:T(8,128)(2,1)}, u32[]{:S(2)}) copy-start(bf16[3,512,512]{2,1,0:T(8,128)(2,1)} %param.9) | copy-start | bytes 4718596
  6.5 28.9 %all-gather.5.cloned.1.call-start = ((), (), s32[]{:S(2)}) async-start(), calls=%async_computation.1 | async-start | bytes 2621440 | tf_op jit(solution)/shard_map/all_gather | solution.py:38
  9.9 142.4 %all-gather.7.cloned.1.call-start = ((), (), s32[]{:S(2)}) async-start(), calls=%async_computation.2 | async-start | bytes 7864320 | tf_op jit(solution)/shard_map/all_gather | solution.py:35
  11.6 175.0 %all-gather.9.cloned.1.call-start = ((), (), s32[]{:S(2)}) async-start(), calls=%async_computation.3 | async-start | bytes 1310720 | tf_op jit(solution)/shard_map/all_gather | solution.py:11
  186.7 1.0 copy-start
  186.7 1.0 copy-start.2
  189.0 2.7 %copy-start.3 = (f32[512]{0:T(512)S(1)}, f32[512]{0:T(512)}, u32[]{:S(2)}) copy-start(f32[512]{0:T(512)} %param.11) | copy-start | bytes 6148
Sparse Core Ops, SparseCore 0:
  10.1 25.2 all-gather.4
  37.0 115.3 all-gather.6
  160.5 26.1 all-gather.8
where the time goes:
time: 211 us
  waiting for transfers between devices  167 us (79%)
  between operations  13.2 us (6%)
  matrix products  11.9 us (6%)
  blocking collectives  11.4 us (5%)
  local copies, waits for them, and re-layouts  3.93 us (2%)
  other arithmetic  3.62 us (2%)
    all_gather x1, waiting for transfers between devices, on_device(): full_weights = lax.all_gather(projections, 'ctx', axis=1, tiled=True)  117 us
    all_gather x1, waiting for transfers between devices, prefix(): gathered = lax.all_gather(part, axis)  26.2 us
    all_gather x1, waiting for transfers between devices, on_device(): lax.all_gather(normed, 'head', axis=0, tiled=True)  23.7 us
    all_to_all x1, blocking collectives, on_device(): lax.all_to_all(result, 'head', split_axis=0, concat_axis=1, tiled=True)  11.4 us
    dot_general x1, matrix products, on_device(): jnp.einsum('td,jdc->jtc', lax.all_gather(normed, 'head', axis=0, tiled=Tr...  6.89 us
  transfers between devices with their start and end apart: 3, of which 3 were waited for; matrix products, arithmetic and copies ran while one was open for 1% of the time, Pallas kernels for 0%

commit v1 on v0

--- a/solution.py
+++ b/solution.py
@@ -4,6 +4,42 @@
 from jax.sharding import PartitionSpec as P
 
 BLOCK = 512
+
+
+def _remake_unit(u_in, link_axis, page):
+    arr_next, carry_out, part_next = (
+        lax.psum(1, link_axis),
+        lax.axis_index(link_axis),
+        u_in.shape[0],
+    )
+    parts_seen = tuple(((k, (k + 1) % arr_next) for k in range(arr_next)))
+    runs = tuple(((src_i, d) for d, src_i in parts_seen))
+    p_next, row_out = (
+        lax.ppermute(u_in, link_axis, parts_seen),
+        lax.ppermute(u_in, link_axis, runs),
+    )
+    all_rows = page(u_in, carry_out * part_next)
+    front = all_rows.shape[1]
+    y_new = jnp.zeros((*all_rows.shape[:1], arr_next * front, *all_rows.shape[2:]), all_rows.dtype)
+
+    def do_the_heaps(y_new, all_rows, arr_now):
+        return lax.dynamic_update_slice_in_dim(y_new, all_rows, arr_now * front, axis=1)
+
+    y_new = do_the_heaps(y_new, all_rows, carry_out)
+    dev = 1
+    while dev < arr_next // 2 + 1:
+        low, outcome_arr = ((carry_out - dev) % arr_next, (carry_out + dev) % arr_next)
+        kept_arr = (p_next, row_out)
+        if dev < arr_next // 2:
+            p_next, row_out = (
+                lax.ppermute(p_next, link_axis, parts_seen),
+                lax.ppermute(row_out, link_axis, runs),
+            )
+        y_new = do_the_heaps(y_new, page(kept_arr[0], low * part_next), low)
+        if 2 * dev < arr_next:
+            y_new = do_the_heaps(y_new, page(kept_arr[1], outcome_arr * part_next), outcome_arr)
+        dev += 1
+    return y_new
 
 
 def prefix(part, axis, combine, identity):
@@ -33,11 +69,12 @@
     heads_here = prior_state.shape[0]
     head_dim = prior_state.shape[1]
     full_weights = lax.all_gather(projections, "ctx", axis=1, tiled=True)
-    mapped = jnp.einsum(
-        "td,jdc->jtc",
-        lax.all_gather(normed, "head", axis=0, tiled=True),
-        full_weights,
-        preferred_element_type=jnp.float32,
+    mapped = _remake_unit(
+        normed,
+        "head",
+        lambda own_block, at: jnp.einsum(
+            "td,jdc->jtc", own_block, full_weights, preferred_element_type=jnp.float32
+        ),
     ).astype(jnp.bfloat16)
     span_rows = mapped.shape[1]
     blocks = span_rows // BLOCK

time: 211 us -> 194 us (0.919)
  waiting for transfers between devices: 167 us -> 140 us
  matrix products: 11.9 us -> 17.4 us
  starting transfers between devices: 0.09 us -> 5.05 us
    all_gather x1 -> x0, waiting for transfers between devices: 23.7 us -> none  [on_device(): lax.all_gather(normed, 'head', axis=0, tiled=True)]
    all_gather x1, waiting for transfers between devices: 117 us -> 103 us  [on_device(): full_weights = lax.all_gather(projections, 'ctx', axis=1, tiled=True)]
    ppermute x0 -> x3, waiting for transfers between devices: none -> 9.76 us  [the longest x1 9.75 us: _remake_unit(): lax.ppermute(u_in, link_axis, parts_seen)]
    dot_general x1 -> x4, matrix products: 6.89 us -> 12.5 us  [on_device(): jnp.einsum('td,jdc->jtc', own_block, full_weights, preferred_element_type...]
    ppermute x0 -> x3, starting transfers between devices: none -> 5.01 us  [the longest x1 2.52 us: _remake_unit(): lax.ppermute(p_next, link_axis, parts_seen)]
  transfers between devices with their start and end apart: 3 -> 5, of which waited for: 3 -> 3; matrix products, arithmetic and copies ran while one was open for 1% -> 6% of each run, Pallas kernels for 0% -> 0%
where the time goes in v1:
time: 194 us
  waiting for transfers between devices  140 us (72%)
  matrix products  17.4 us (9%)
  between operations  13.6 us (7%)
  blocking collectives  11.4 us (6%)
  starting transfers between devices  5.05 us (3%)
  local copies, waits for them, and re-layouts  4.4 us (2%)
    all_gather x1, waiting for transfers between devices, on_device(): full_weights = lax.all_gather(projections, 'ctx', axis=1, tiled=True)  103 us
    all_gather x1, waiting for transfers between devices, prefix(): gathered = lax.all_gather(part, axis)  26.2 us
    dot_general x4, matrix products, on_device(): jnp.einsum('td,jdc->jtc', own_block, full_weights, preferred_element_type...  12.5 us
    all_to_all x1, blocking collectives, on_device(): lax.all_to_all(result, 'head', split_axis=0, concat_axis=1, tiled=True)  11.4 us
    ppermute x1, waiting for transfers between devices, _remake_unit(): lax.ppermute(u_in, link_axis, parts_seen)  9.75 us
  transfers between devices with their start and end apart: 5, of which 3 were waited for; matrix products, arithmetic and copies ran while one was open for 6% of the time, Pallas kernels for 0%

profile of v1, /device:TPU:0, one launch (start us, length us, event | category | flops | bytes accessed | tf_op | source)
XLA Modules:
  0.0 193.7 jit_solution(5936233142773895514)
XLA Ops:
  6.5 0.0 copy-start.2
  6.5 0.0 copy-start.4
  6.5 0.0 all-gather.4.cloned.1.call-start
  6.5 0.7 all-gather.4.cloned.1.call-update
  7.3 0.0 all-gather.6.cloned.1.call-start
  7.3 1.2 fusion.3
  8.5 0.0 copy-done.2
  8.6 0.0 copy-done.4
  8.6 0.2 fusion.5
  8.8 0.5 collective-permute-start
  9.3 2.0 %collective-permute-start.1 = (bf16[128,2048]{1,0:T(8,128)(2,1)S(1)}, bf16[128,2048]{1,0:T(8,128)(2,1)S(1)}, u32[]{:S(2)}, u32[]{:S(2)}) collective-permute-start(bf16[128,2048]{1,0:T(8,128)(2,1)S(1)} %fusion.5), channel_id=1, source_target_pairs={{1,0},{2,1},{3,2},{0,3},{5,4},{6,5},{7,6},{4,7},{9,8},{10,9},{11,1... | collective-permute-start | bytes 1572872 | tf_op jit(solution)/shard_map/ppermute | solution.py:19
  11.3 9.8 %collective-permute-done = bf16[128,2048]{1,0:T(8,128)(2,1)S(1)} collective-permute-done((bf16[128,2048]{1,0:T(8,128)(2,1)S(1)}, bf16[128,2048]{1,0:T(8,128)(2,1)S(1)}, u32[]{:S(2)}, u32[]{:S(2)}) %collective-permute-start) | collective-permute-done | bytes 524320 | tf_op jit(solution)/shard_map/ppermute | solution.py:18
  21.0 2.5 %collective-permute-start.2 = (bf16[128,2048]{1,0:T(8,128)(2,1)S(1)}, bf16[128,2048]{1,0:T(8,128)(2,1)S(1)}, u32[]{:S(2)}, u32[]{:S(2)}) collective-permute-start(bf16[128,2048]{1,0:T(8,128)(2,1)S(1)} %collective-permute-done), channel_id=1, source_target_pairs={{0,1},{1,2},{2,3},{3,0},{4,5},{5,6},{6,7},{7,4},{8,9},{9,10},{10,1... | collective-permute-start | bytes 1572872 | tf_op jit(solution)/shard_map/ppermute | solution.py:35
  23.5 103.5 %all-gather.4.cloned.1.call-done = bf16[3,2048,512]{2,1,0:T(8,128)(2,1)} async-done(((bf16[3,512,512]{2,1,0:T(8,128)(2,1)}), bf16[3,2048,512]{2,1,0:T(8,128)(2,1)}) %all-gather.4.cloned.1.call-update) | async-done | bytes 6291472 | tf_op jit(solution)/shard_map/all_gather | solution.py:71
  127.0 0.0 copy-start
  127.0 3.9 %convolution_bitcast_fusion.3 = bf16[3,128,512]{2,1,0:T(8,128)(2,1)S(1)} fusion(bf16[3,2048,512]{2,1,0:T(8,128)(2,1)} %all-gather.4.cloned.1.call-done, bf16[128,2048]{1,0:T(8,128)(2,1)S(1)} %fusion.5), kind=kOutput, calls=%fused_computation.10 | convolution fusion | flops 805306368 | bytes 7208960 | tf_op jit(solution)/shard_map/td,jdc->jtc/dot_general | solution.py:75
  130.9 0.0 collective-permute-done.1
  131.0 0.7 copy-done
  131.6 1.0 convolution_bitcast_fusion.1
  132.6 0.2 copy.33
  132.8 0.2 copy.35
  133.1 3.8 %convolution_bitcast_fusion.2 = bf16[3,128,512]{2,1,0:T(8,128)(2,1)S(1)} fusion(bf16[3,2048,512]{2,1,0:T(8,128)(2,1)} %all-gather.4.cloned.1.call-done, bf16[128,2048]{1,0:T(8,128)(2,1)S(1)} %collective-permute-done), kind=kOutput, calls=%fused_computation.9 | convolution fusion | flops 805306368 | bytes 7208960 | tf_op jit(solution)/shard_map/td,jdc->jtc/dot_general | solution.py:75
  136.9 0.2 copy.34
  137.1 0.0 collective-permute-done.2
  137.1 3.8 %convolution_bitcast_fusion = bf16[3,128,512]{2,1,0:T(8,128)(2,1)S(1)} fusion(bf16[3,2048,512]{2,1,0:T(8,128)(2,1)} %all-gather.4.cloned.1.call-done, bf16[128,2048]{1,0:T(8,128)(2,1)S(1)} %collective-permute-done.2), kind=kOutput, calls=%fused_computation.7 | convolution fusion | flops 805306368 | bytes 7208960 | tf_op jit(solution)/shard_map/td,jdc->jtc/dot_general | solution.py:75
  140.9 0.2 copy.36
  141.1 0.1 broadcast_in_dim.16
  141.2 0.1 constant_dynamic-update-slice_fusion.3
  141.3 0.1 constant_dynamic-update-slice_fusion.2
  141.4 0.1 constant_dynamic-update-slice_fusion.1
  141.6 0.1 constant_dynamic-update-slice_fusion
  141.7 0.1 fusion.14
  141.8 1.0 fusion.15
  142.8 0.0 all-gather.6.cloned.1.call-update
  142.8 0.1 iota_compare_fusion
  142.9 26.2 %all-gather.6.cloned.1.call-done = f32[16,128,128]{2,1,0:T(8,128)} async-done(((f32[4,128,128]{2,1,0:T(8,128)}), f32[16,128,128]{2,1,0:T(8,128)}) %all-gather.6.cloned.1.call-update) | async-done | bytes 1048592 | tf_op jit(solution)/shard_map/all_gather | solution.py:47
  169.1 0.0 copy-start.1
  169.1 0.0 copy-start.3
  169.1 0.9 copy-done.1
  170.1 0.1 copy-done.3
  170.1 1.3 fusion.11
  171.5 0.0 copy-start.5
  171.5 2.6 %multiply_reduce_fusion = (f32[512,4]{0,1:T(4,128)S(1)}, f32[1,512,4,128]{1,3,2,0:T(8,128)S(1)}) fusion(f32[4,128,512]{2,1,0:T(8,128)} %fusion.11, bf16[512,4,128]{0,2,1:T(8,128)(2,1)S(1)} %bitcast.52, bf16[512,4,128]{0,2,1:T(8,128)(2,1)S(1)} %bitcast.56, bf16[512,4,128]{0,2,1:T(8,128)(2,1)S(1)} %bitcast.54, pred[512,512]{1,0:T(8,128)(4,1)S(1)} %iota_compare_fusion), kind=kOutput, calls=%fused_computation.15 | convolution fusion | flops 539752448 | bytes 3940352 | tf_op jit(solution)/shard_map/bhqk,bkhd->bqhd/dot_general | solution.py:96
  174.1 0.0 copy-done.5
  174.1 0.2 multiply_convert_fusion
  174.3 0.1 all_to_all.14
  174.4 0.1 copy.42
  174.5 11.4 %all_to_all.19 = bf16[4,128,512]{1,2,0:T(8,128)(2,1)S(1)} all-to-all(bf16[4,128,512]{1,2,0:T(8,128)(2,1)S(1)} %copy.42), channel_id=1, replica_groups=mesh['runs'=2,'ctx'=4,'head'=4] {'head'}, dimensions={0} | all-to-all | bytes 1048576 | tf_op jit(solution)/shard_map/all_to_all | solution.py:104
  185.9 1.0 copy.43
  (4 shorter events, 0.0 us)
Async XLA Ops:
  6.5 2.0 %copy-start.2 = (bf16[128,2048]{1,0:T(8,128)(2,1)S(1)}, bf16[128,2048]{1,0:T(8,128)(2,1)}, u32[]{:S(2)}) copy-start(bf16[128,2048]{1,0:T(8,128)(2,1)} %param.7) | copy-start | bytes 1572868
  6.5 2.0 %copy-start.4 = (f32[2048]{0:T(1024)S(1)}, f32[2048]{0:T(1024)}, u32[]{:S(2)}) copy-start(f32[2048]{0:T(1024)} %param.8) | copy-start | bytes 24580
  6.5 120.5 %all-gather.4.cloned.1.call-start = ((), (), s32[]{:S(2)}) async-start(), calls=%async_computation.1 | async-start | bytes 7864320 | tf_op jit(solution)/shard_map/all_gather | solution.py:71
  7.3 161.8 %all-gather.6.cloned.1.call-start = ((), (), s32[]{:S(2)}) async-start(), calls=%async_computation.2 | async-start | bytes 1310720 | tf_op jit(solution)/shard_map/all_gather | solution.py:47
  8.8 12.2 %collective-permute-start = (bf16[128,2048]{1,0:T(8,128)(2,1)S(1)}, bf16[128,2048]{1,0:T(8,128)(2,1)S(1)}, u32[]{:S(2)}, u32[]{:S(2)}) collective-permute-start(bf16[128,2048]{1,0:T(8,128)(2,1)S(1)} %fusion.5), channel_id=1, source_target_pairs={{0,1},{1,2},{2,3},{3,0},{4,5},{5,6},{6,7},{7,4},{8,9},{9,10},{10,1... | collective-permute-start | bytes 1572872 | tf_op jit(solution)/shard_map/ppermute | solution.py:18
  9.3 121.7 %collective-permute-start.1 = (bf16[128,2048]{1,0:T(8,128)(2,1)S(1)}, bf16[128,2048]{1,0:T(8,128)(2,1)S(1)}, u32[]{:S(2)}, u32[]{:S(2)}) collective-permute-start(bf16[128,2048]{1,0:T(8,128)(2,1)S(1)} %fusion.5), channel_id=1, source_target_pairs={{1,0},{2,1},{3,2},{0,3},{5,4},{6,5},{7,6},{4,7},{9,8},{10,9},{11,1... | collective-permute-start | bytes 1572872 | tf_op jit(solution)/shard_map/ppermute | solution.py:19
  21.0 116.1 %collective-permute-start.2 = (bf16[128,2048]{1,0:T(8,128)(2,1)S(1)}, bf16[128,2048]{1,0:T(8,128)(2,1)S(1)}, u32[]{:S(2)}, u32[]{:S(2)}) collective-permute-start(bf16[128,2048]{1,0:T(8,128)(2,1)S(1)} %collective-permute-done), channel_id=1, source_target_pairs={{0,1},{1,2},{2,3},{3,0},{4,5},{5,6},{6,7},{7,4},{8,9},{9,10},{10,1... | collective-permute-start | bytes 1572872 | tf_op jit(solution)/shard_map/ppermute | solution.py:35
  127.0 4.6 %copy-start = (bf16[3,2048,512]{2,1,0:T(8,128)(2,1)S(1)}, bf16[3,2048,512]{2,1,0:T(8,128)(2,1)}, u32[]{:S(2)}) copy-start(bf16[3,2048,512]{2,1,0:T(8,128)(2,1)} %all-gather.4.cloned.1.call-done) | copy-start | bytes 18874372
  169.1 1.0 copy-start.1
  169.1 1.0 copy-start.3
  171.5 2.7 %copy-start.5 = (f32[512]{0:T(512)S(1)}, f32[512]{0:T(512)}, u32[]{:S(2)}) copy-start(f32[512]{0:T(512)} %param.11) | copy-start | bytes 6148
Sparse Core Ops, SparseCore 0:
  8.9 118.0 all-gather.3
  142.9 26.1 all-gather.5
